TPU v7x, 32 devices: a whole 2x2x4 slice. The times are simulated.
32 devices in a mesh: groups: 2 (over x), seq: 8 (over z, y), head: 2 (over core).
Axes of the slice: x: 2, y: 2, z: 4, core: 2. Of those that a mesh axis runs over, the one named last changes fastest.
Arguments:
- queries: bfloat16 [8192, 2048], P(('groups', 'seq'), 'head'), parts along dimension 0, may hold values from -6 to 6
- keys: bfloat16 [8192, 1024], P(('groups', 'seq'), 'head'), parts along dimension 0, may hold values from -6 to 6
- values: bfloat16 [8192, 1024], P(('groups', 'seq'), 'head'), parts along dimension 0, may hold values from -6 to 6
- segments: int32 [8192], P('groups'), parts along dimension 0, may hold values from 0 to 7, never falling along the last dimension, each value on 1 to 1024 neighbouring positions
- out_weight: bfloat16 [2048, 5376], P('head'), may hold values from -0.125 to 0.125
Outputs:
- mixed: bfloat16 [8192, 5376], P(('groups', 'seq')), parts along dimension 0
There are 2 independent parts, one for each index of `groups`. A program takes and returns all parts, laid end to end along the dimension named above; an argument that names none is the same for every part. Nothing has to cross between parts.
Inputs may be any that keep to these rules, and one draw needn't show every extreme that they name: `segments`: document ids never fall along the slab; each document has 1 to 1024 tokens, one exactly 1024.
All inputs are finite; a program needn't handle non-finite values.
Results may differ from a plain program's by a relative error of at most 0.011.
Values may be sent and summed in bfloat16 or wider, within the bound.
A program may use at most 128 MiB of HBM per device.

v0:
```python
import math
import jax
import jax.numpy as jnp
from jax import lax
from jax.sharding import PartitionSpec as P

HEAD_SIZE = 128
SCALAR = 168
ATTENTION_SPAN = 1024
HALO = 2


def from_behind(value, axis, by):
    peers = lax.axis_size(axis)
    pairs = [(i, i + by) for i in range(peers) if 0 <= i + by < peers]
    return lax.ppermute(value, axis, pairs)


def shards(queries, keys, values, segments, out_weight):
    tok_rows = queries.shape[0]
    heads_kv = keys.shape[1] // HEAD_SIZE
    query_group = queries.shape[1] // keys.shape[1]
    seq_index = lax.axis_index("seq")
    pieces = []
    for distance in range(HALO, 0, -1):
        pieces.append(from_behind((keys, values), "seq", distance))
    keys_ext = jnp.concatenate([piece[0] for piece in pieces] + [keys], axis=0)
    values_ext = jnp.concatenate([piece[1] for piece in pieces] + [values], axis=0)
    window_span = keys_ext.shape[0]
    first_row = seq_index * tok_rows
    pad_segments = jnp.concatenate([jnp.full((HALO * tok_rows,), -1, jnp.int32), segments])
    seg_key = lax.dynamic_slice_in_dim(pad_segments, first_row, window_span, 0)
    seg_query = lax.dynamic_slice_in_dim(segments, first_row, tok_rows, 0)
    key_pos = first_row - HALO * tok_rows + jnp.arange(window_span, dtype=jnp.int32)
    key_mat = keys_ext.reshape(window_span, heads_kv, HEAD_SIZE)
    value_mat = values_ext.reshape(window_span, heads_kv, HEAD_SIZE)
    token_block = math.gcd(tok_rows, 512)

    def one_block(block_id):
        start = block_id * token_block
        query_block = queries.reshape(token_block, heads_kv, query_group, HEAD_SIZE)
        query_pos = first_row + start + jnp.arange(token_block, dtype=jnp.int32)
        allowed = (
            (key_pos[None, :] <= query_pos[:, None])
            & (query_pos[:, None] - key_pos[None, :] < ATTENTION_SPAN)
            & (seg_key[None, :] == seg_query[:, None])
        )
        scores = jnp.einsum(
            "qkgd,pkd->kgqp", query_block, key_mat, preferred_element_type=jnp.float32
        ) * SCALAR ** (-0.5)
        masked = jnp.where(allowed, scores, -1e30)
        row_max = jnp.max(masked, axis=-1, keepdims=True)
        expo = jnp.where(allowed, jnp.exp(masked - row_max), 0.0)
        weights = (expo / jnp.sum(expo, axis=-1, keepdims=True)).astype(jnp.bfloat16)
        heads_out = jnp.einsum(
            "kgqp,pkd->qkgd", weights, value_mat, preferred_element_type=jnp.float32
        )
        return heads_out.astype(jnp.bfloat16).reshape(
            token_block, heads_kv * query_group * HEAD_SIZE
        )

    attended = lax.map(one_block, jnp.arange(tok_rows // token_block, dtype=jnp.int32)).reshape(
        tok_rows, -1
    )
    partial_terms = jnp.dot(attended, out_weight, preferred_element_type=jnp.float32)
    mixed = lax.psum(partial_terms, "head").astype(jnp.bfloat16)
    return mixed


def solution(mesh):
    placed = (
        P(("groups", "seq"), "head"),
        P(("groups", "seq"), "head"),
        P(("groups", "seq"), "head"),
        P("groups"),
        P("head", None),
    )
    return jax.shard_map(
        shards, mesh=mesh, in_specs=placed, out_specs=P(("groups", "seq"), None), check_vma=False
    )
```

profile of v0, /device:TPU:17, one launch (start us, length us, event | category | flops | bytes accessed | tf_op | source)
XLA Modules:
  0.0 131.4 jit_solution(17479699707473325721)
XLA Ops:
  0.0 1.3 copy.10
  1.3 3.1 %collective-permute-start.3 = (bf16[512,512]{0,1:T(8,128)(2,1)S(1)}, bf16[512,512]{0,1:T(8,128)(2,1)}, u32[]{:S(2)}, u32[]{:S(2)}) collective-permute-start(bf16[512,512]{0,1:T(8,128)(2,1)S(1)} %copy.10), channel_id=1, source_target_pairs={{0,2},{2,4},{4,6},{6,8},{8,10},{10,12},{12,14},{1,3},{3,5},{5,7},{... | collective-permute-start | bytes 1572872 | tf_op jit(solution)/shard_map/ppermute | solution.py:16
  4.4 3.2 %collective-permute-start.2 = (bf16[512,512]{0,1:T(8,128)(2,1)S(1)}, bf16[512,512]{0,1:T(8,128)(2,1)}, u32[]{:S(2)}, u32[]{:S(2)}) collective-permute-start(bf16[512,512]{0,1:T(8,128)(2,1)S(1)} %copy.10), channel_id=1, source_target_pairs={{0,4},{2,6},{4,8},{6,10},{8,12},{10,14},{1,5},{3,7},{5,9},{7,11},{... | collective-permute-start | bytes 1572872 | tf_op jit(solution)/shard_map/ppermute | solution.py:16
  7.6 1.9 %collective-permute-start = (bf16[512,512]{1,0:T(8,128)(2,1)}, bf16[512,512]{1,0:T(8,128)(2,1)S(1)}, u32[]{:S(2)}, u32[]{:S(2)}) collective-permute-start(bf16[512,512]{1,0:T(8,128)(2,1)} %param.7), channel_id=1, source_target_pairs={{0,4},{2,6},{4,8},{6,10},{8,12},{10,14},{1,5},{3,7},{5,9},{7,11},{... | collective-permute-start | bytes 1572872 | tf_op jit(solution)/shard_map/ppermute | solution.py:16
  9.6 1.9 %collective-permute-start.1 = (bf16[512,512]{1,0:T(8,128)(2,1)}, bf16[512,512]{1,0:T(8,128)(2,1)}, u32[]{:S(2)}, u32[]{:S(2)}) collective-permute-start(bf16[512,512]{1,0:T(8,128)(2,1)} %param.7), channel_id=1, source_target_pairs={{0,2},{2,4},{4,6},{6,8},{8,10},{10,12},{12,14},{1,3},{3,5},{5,7},{... | collective-permute-start | bytes 1572872 | tf_op jit(solution)/shard_map/ppermute | solution.py:16
  11.5 0.8 pad_dynamic-slice_fusion
  12.3 0.8 dynamic_slice.10
  13.1 1.9 %fusion.9 = pred[512,1536]{0,1:T(8,128)(4,1)} fusion(s32[512]{0:T(512)S(1)} %dynamic_slice.10, s32[512]{0:T(512)S(1)} %iota_add_fusion.1, s32[1536]{0:T(1024)S(1)} %get-tuple-element.21, s32[1536]{0:T(1024)S(1)} %get-tuple-element.22), kind=kLoop, calls=%fused_computation.12 | loop fusion | flops 4718592 | bytes 802816 | tf_op jit(solution)/shard_map/while/body/eval_jaxpr/and | solution.py:44
  14.9 1.8 %reshape.31 = bf16[512,4,2,128]{3,2,1,0:T(2,128)(2,1)S(1)} reshape(bf16[512,1024]{1,0:T(8,128)(2,1)} %param.5) | data formatting | bytes 2097152 | tf_op jit(solution)/shard_map/while/body/eval_jaxpr/reshape | solution.py:41
  16.7 0.0 copy-start.1
  16.7 13.3 %collective-permute-done = bf16[512,512]{1,0:T(8,128)(2,1)S(1)} collective-permute-done((bf16[512,512]{1,0:T(8,128)(2,1)}, bf16[512,512]{1,0:T(8,128)(2,1)S(1)}, u32[]{:S(2)}, u32[]{:S(2)}) %collective-permute-start) | collective-permute-done | bytes 524320 | tf_op jit(solution)/shard_map/ppermute | solution.py:16
  30.1 0.0 copy-start.2
  30.1 0.8 copy-done.2
  30.9 19.8 %collective-permute-done.1 = bf16[512,512]{1,0:T(8,128)(2,1)} collective-permute-done((bf16[512,512]{1,0:T(8,128)(2,1)}, bf16[512,512]{1,0:T(8,128)(2,1)}, u32[]{:S(2)}, u32[]{:S(2)}) %collective-permute-start.1) | collective-permute-done | bytes 524320 | tf_op jit(solution)/shard_map/ppermute | solution.py:16
  50.7 1.5 %pad_maximum_fusion = bf16[1536,512]{1,0:T(8,128)(2,1)S(1)} fusion(bf16[512,512]{1,0:T(8,128)(2,1)} %param.7, bf16[512,512]{1,0:T(8,128)(2,1)} %collective-permute-done.1, bf16[512,512]{1,0:T(8,128)(2,1)} %copy-done.2), kind=kLoop, calls=%fused_computation.13 | loop fusion | flops 4718592 | bytes 3145728 | tf_op jit(solution)/shard_map/concatenate | solution.py:28
  52.1 1.6 %copy.9 = bf16[1536,512]{0,1:T(8,128)(2,1)} copy(bf16[1536,512]{1,0:T(8,128)(2,1)S(1)} %pad_maximum_fusion) | data formatting | bytes 3145728 | tf_op jit(solution)/shard_map/concatenate | solution.py:28
  53.7 0.0 collective-permute-done.3
  53.7 0.0 collective-permute-done.2
  53.7 2.5 %pad_maximum_fusion.1 = bf16[1536,512]{0,1:T(8,128)(2,1)} fusion(bf16[512,512]{0,1:T(8,128)(2,1)S(1)} %copy.10, bf16[512,512]{0,1:T(8,128)(2,1)} %collective-permute-done.3, bf16[512,512]{0,1:T(8,128)(2,1)} %collective-permute-done.2), kind=kLoop, calls=%fused_computation.14 | loop fusion | flops 4718592 | bytes 3145728 | tf_op jit(solution)/shard_map/concatenate | solution.py:27
  56.2 0.0 copy-done.1
  56.2 0.0 copy-start
  56.2 13.4 %fusion.28 = f32[4,2,512]{2,1,0:T(2,128)S(1)} fusion(pred[512,1536]{0,1:T(8,128)(4,1)} %fusion.9, bf16[1536,4,128,1]{0,2,3,1:T(8,128)(2,1)} %bitcast.32, bf16[512,4,2,128]{3,2,1,0:T(2,128)(2,1)S(1)} %reshape.31), kind=kOutput, calls=%fused_computation.29 | convolution fusion | flops 1642071552 | bytes 3424256 | tf_op jit(solution)/shard_map/while/body/eval_jaxpr/sub | solution.py:53
  69.6 0.0 copy-done
  69.6 15.7 %fusion.10 = bf16[4,128,2,512]{3,1,2,0:T(8,128)(2,1)S(1)} fusion(bf16[1536,4,128,1]{0,2,3,1:T(8,128)(2,1)S(1)} %bitcast.31, f32[4,2,512]{2,1,0:T(2,128)S(1)} %fusion.28, pred[512,1536]{0,1:T(8,128)(4,1)} %fusion.9, bf16[1536,4,128,1]{0,2,3,1:T(8,128)(2,1)} %bitcast.33, bf16[512,4,2,128]{3,2,1,0:T(2,128)(2,1)} %copy-done.1), kind=kOutput, calls=%fused_computation.15 | convolution fusion | flops 3259504128 | bytes 6045696 | tf_op jit(solution)/shard_map/while/body/eval_jaxpr/kgqp,pkd->qkgd/dot_general | solution.py:55
  85.4 12.7 %fusion.31 = f32[512,5376]{1,0:T(8,128)} fusion(bf16[512,1024]{0,1:T(8,128)(2,1)S(1)} %bitcast.34, bf16[1024,5376]{1,0:T(8,128)(2,1)} %param.9), kind=kOutput, calls=%fused_computation.30 | convolution fusion | flops 5637144576 | bytes 23068672 | tf_op jit(solution)/shard_map/dot_general | solution.py:65
  98.1 33.3 %all-reduce.2 = bf16[512,5376]{1,0:T(8,128)(2,1)} all-reduce(f32[512,5376]{1,0:T(8,128)} %fusion.31), channel_id=1, replica_groups=mesh['groups'=2,'seq'=8,'head'=2] {'head'}, use_global_device_ids=true, to_apply=%region_2.3 | all-reduce | flops 2752512 | bytes 16515072 | tf_op jit(solution)/shard_map/psum | solution.py:66
  (1 shorter events, 0.0 us)
Async XLA Ops:
  1.3 52.5 %collective-permute-start.3 = (bf16[512,512]{0,1:T(8,128)(2,1)S(1)}, bf16[512,512]{0,1:T(8,128)(2,1)}, u32[]{:S(2)}, u32[]{:S(2)}) collective-permute-start(bf16[512,512]{0,1:T(8,128)(2,1)S(1)} %copy.10), channel_id=1, source_target_pairs={{0,2},{2,4},{4,6},{6,8},{8,10},{10,12},{12,14},{1,3},{3,5},{5,7},{... | collective-permute-start | bytes 1572872 | tf_op jit(solution)/shard_map/ppermute | solution.py:16
  4.4 49.3 %collective-permute-start.2 = (bf16[512,512]{0,1:T(8,128)(2,1)S(1)}, bf16[512,512]{0,1:T(8,128)(2,1)}, u32[]{:S(2)}, u32[]{:S(2)}) collective-permute-start(bf16[512,512]{0,1:T(8,128)(2,1)S(1)} %copy.10), channel_id=1, source_target_pairs={{0,4},{2,6},{4,8},{6,10},{8,12},{10,14},{1,5},{3,7},{5,9},{7,11},{... | collective-permute-start | bytes 1572872 | tf_op jit(solution)/shard_map/ppermute | solution.py:16
  7.6 22.4 %collective-permute-start = (bf16[512,512]{1,0:T(8,128)(2,1)}, bf16[512,512]{1,0:T(8,128)(2,1)S(1)}, u32[]{:S(2)}, u32[]{:S(2)}) collective-permute-start(bf16[512,512]{1,0:T(8,128)(2,1)} %param.7), channel_id=1, source_target_pairs={{0,4},{2,6},{4,8},{6,10},{8,12},{10,14},{1,5},{3,7},{5,9},{7,11},{... | collective-permute-start | bytes 1572872 | tf_op jit(solution)/shard_map/ppermute | solution.py:16
  9.6 41.1 %collective-permute-start.1 = (bf16[512,512]{1,0:T(8,128)(2,1)}, bf16[512,512]{1,0:T(8,128)(2,1)}, u32[]{:S(2)}, u32[]{:S(2)}) collective-permute-start(bf16[512,512]{1,0:T(8,128)(2,1)} %param.7), channel_id=1, source_target_pairs={{0,2},{2,4},{4,6},{6,8},{8,10},{10,12},{12,14},{1,3},{3,5},{5,7},{... | collective-permute-start | bytes 1572872 | tf_op jit(solution)/shard_map/ppermute | solution.py:16
  16.7 39.4 %copy-start.1 = (bf16[512,4,2,128]{3,2,1,0:T(2,128)(2,1)}, bf16[512,4,2,128]{3,2,1,0:T(2,128)(2,1)S(1)}, u32[]{:S(2)}) copy-start(bf16[512,4,2,128]{3,2,1,0:T(2,128)(2,1)S(1)} %reshape.31) | copy-start | bytes 3145732
  30.1 0.8 copy-start.2
  56.2 13.4 %copy-start = (bf16[1536,512]{0,1:T(8,128)(2,1)S(1)}, bf16[1536,512]{0,1:T(8,128)(2,1)}, u32[]{:S(2)}) copy-start(bf16[1536,512]{0,1:T(8,128)(2,1)} %copy.9) | copy-start | bytes 4718596
where the time goes:
time: 132 us; the launch traced here: 131 us
  matrix products  41.9 us (32%)
  blocking collectives  33.3 us (25%)
  waiting for transfers between devices  33.1 us (25%)
  starting transfers between devices  10.2 us (8%)
  other arithmetic  6.6 us (5%)
  local copies, waits for them, and re-layouts  6.17 us (5%)
    psum x1, blocking collectives, shards(): mixed = lax.psum(partial_terms, 'head').astype(jnp.bfloat16)  33.3 us
    ppermute x4, waiting for transfers between devices, from_behind(): return lax.ppermute(value, axis, pairs)  33.1 us
    dot_general x1, matrix products, one_block(): jnp.einsum('kgqp,pkd->qkgd', weights, value_mat, preferred_element_type=j...  15.7 us
    sub x1, matrix products, one_block(): expo = jnp.where(allowed, jnp.exp(masked - row_max), 0.0)  13.4 us
    dot_general x1, matrix products, shards(): jnp.dot(attended, out_weight, preferred_element_type=jnp.float32)  12.7 us
    ppermute x4, starting transfers between devices, from_behind(): return lax.ppermute(value, axis, pairs)  10.2 us
  transfers between devices with their start and end apart: 4, of which 2 were waited for; matrix products, arithmetic and copies ran while one was open for 6% of the time, Pallas kernels for 0%

commit v1 on v0

--- a/solution.py
+++ b/solution.py
@@ -63,7 +63,7 @@
         tok_rows, -1
     )
     partial_terms = jnp.dot(attended, out_weight, preferred_element_type=jnp.float32)
-    mixed = lax.psum(partial_terms, "head").astype(jnp.bfloat16)
+    mixed = jnp.sum(lax.all_gather(partial_terms, "head"), axis=0).astype(jnp.bfloat16)
     return mixed
 
 

time: 132 us -> 163 us (1.23)
  waiting for transfers between devices: 33.1 us -> 70.9 us
  blocking collectives: 33.3 us -> 0 us
  between operations: 0.09 us -> 13.5 us
  other arithmetic: 6.6 us -> 17.8 us
  local copies, waits for them, and re-layouts: 6.17 us -> 7.85 us
    all_gather x0 -> x1, waiting for transfers between devices: none -> 38.5 us  [shards(): lax.all_gather(partial_terms, 'head')]
    psum x1 -> x0, blocking collectives: 33.3 us -> none  [shards(): mixed = lax.psum(partial_terms, 'head').astype(jnp.bfloat16)]
    reduce_sum x0 -> x1, other arithmetic: none -> 12.5 us  [shards(): jnp.sum(lax.all_gather(partial_terms, 'head'), axis=0).astype(jnp.bfloat16)]
  transfers between devices with their start and end apart: 4 -> 5, of which waited for: 2 -> 3; matrix products, arithmetic and copies ran while one was open for 6% -> 6% of each run, Pallas kernels for 0% -> 0%
where the time goes in v1:
time: 163 us; the launch traced here: 161 us
  waiting for transfers between devices  70.9 us (43%)
  matrix products  41.2 us (25%)
  other arithmetic  17.8 us (11%)
  between operations  13.5 us (8%)
  starting transfers between devices  10.2 us (6%)
  local copies, waits for them, and re-layouts  7.85 us (5%)
    all_gather x1, waiting for transfers between devices, shards(): lax.all_gather(partial_terms, 'head')  38.5 us
    ppermute x4, waiting for transfers between devices, from_behind(): return lax.ppermute(value, axis, pairs)  32.4 us
    dot_general x1, matrix products, one_block(): jnp.einsum('kgqp,pkd->qkgd', weights, value_mat, preferred_element_type=j...  16.3 us
    dot_general x1, matrix products, shards(): jnp.dot(attended, out_weight, preferred_element_type=jnp.float32)  12.8 us
    reduce_sum x1, other arithmetic, shards(): jnp.sum(lax.all_gather(partial_terms, 'head'), axis=0).astype(jnp.bfloat16)  12.5 us
    sub x1, matrix products, one_block(): expo = jnp.where(allowed, jnp.exp(masked - row_max), 0.0)  12.1 us
    ppermute x4, starting transfers between devices, from_behind(): return lax.ppermute(value, axis, pairs)  10.2 us
  transfers between devices with their start and end apart: 5, of which 3 were waited for; matrix products, arithmetic and copies ran while one was open for 6% of the time, Pallas kernels for 0%

profile of v1, /device:TPU:17, one launch (start us, length us, event | category | flops | bytes accessed | tf_op | source)
XLA Modules:
  0.0 161.4 jit_solution(18055654217611041493)
XLA Ops:
  6.5 0.0 copy-start.1
  6.5 0.0 all-gather.3.cloned.1.call-start
  6.5 1.3 copy.10
  7.9 3.1 %collective-permute-start.3 = (bf16[512,512]{0,1:T(8,128)(2,1)S(1)}, bf16[512,512]{0,1:T(8,128)(2,1)S(1)}, u32[]{:S(2)}, u32[]{:S(2)}) collective-permute-start(bf16[512,512]{0,1:T(8,128)(2,1)S(1)} %copy.10), channel_id=1, source_target_pairs={{0,2},{2,4},{4,6},{6,8},{8,10},{10,12},{12,14},{1,3},{3,5},{5,7},{... | collective-permute-start | bytes 1572872 | tf_op jit(solution)/shard_map/ppermute | solution.py:16
  11.0 3.2 %collective-permute-start.2 = (bf16[512,512]{0,1:T(8,128)(2,1)S(1)}, bf16[512,512]{0,1:T(8,128)(2,1)}, u32[]{:S(2)}, u32[]{:S(2)}) collective-permute-start(bf16[512,512]{0,1:T(8,128)(2,1)S(1)} %copy.10), channel_id=1, source_target_pairs={{0,4},{2,6},{4,8},{6,10},{8,12},{10,14},{1,5},{3,7},{5,9},{7,11},{... | collective-permute-start | bytes 1572872 | tf_op jit(solution)/shard_map/ppermute | solution.py:16
  14.2 1.9 %collective-permute-start = (bf16[512,512]{1,0:T(8,128)(2,1)}, bf16[512,512]{1,0:T(8,128)(2,1)S(1)}, u32[]{:S(2)}, u32[]{:S(2)}) collective-permute-start(bf16[512,512]{1,0:T(8,128)(2,1)} %param.7), channel_id=1, source_target_pairs={{0,4},{2,6},{4,8},{6,10},{8,12},{10,14},{1,5},{3,7},{5,9},{7,11},{... | collective-permute-start | bytes 1572872 | tf_op jit(solution)/shard_map/ppermute | solution.py:16
  16.2 1.9 %collective-permute-start.1 = (bf16[512,512]{1,0:T(8,128)(2,1)}, bf16[512,512]{1,0:T(8,128)(2,1)}, u32[]{:S(2)}, u32[]{:S(2)}) collective-permute-start(bf16[512,512]{1,0:T(8,128)(2,1)} %param.7), channel_id=1, source_target_pairs={{0,2},{2,4},{4,6},{6,8},{8,10},{10,12},{12,14},{1,3},{3,5},{5,7},{... | collective-permute-start | bytes 1572872 | tf_op jit(solution)/shard_map/ppermute | solution.py:16
  18.1 0.8 pad_dynamic-slice_fusion
  18.9 0.8 dynamic_slice.10
  19.6 1.9 %fusion.9 = pred[512,1536]{0,1:T(8,128)(4,1)} fusion(s32[512]{0:T(512)S(1)} %dynamic_slice.10, s32[512]{0:T(512)S(1)} %iota_add_fusion.1, s32[1536]{0:T(1024)S(1)} %get-tuple-element.21, s32[1536]{0:T(1024)S(1)} %get-tuple-element.22), kind=kLoop, calls=%fused_computation.12 | loop fusion | flops 4718592 | bytes 802816 | tf_op jit(solution)/shard_map/while/body/eval_jaxpr/and | solution.py:44
  21.5 2.6 %reshape.31 = bf16[512,4,2,128]{3,2,1,0:T(2,128)(2,1)} reshape(bf16[512,1024]{1,0:T(8,128)(2,1)} %param.5) | data formatting | bytes 2097152 | tf_op jit(solution)/shard_map/while/body/eval_jaxpr/reshape | solution.py:41
  24.1 12.6 %collective-permute-done = bf16[512,512]{1,0:T(8,128)(2,1)S(1)} collective-permute-done((bf16[512,512]{1,0:T(8,128)(2,1)}, bf16[512,512]{1,0:T(8,128)(2,1)S(1)}, u32[]{:S(2)}, u32[]{:S(2)}) %collective-permute-start) | collective-permute-done | bytes 524320 | tf_op jit(solution)/shard_map/ppermute | solution.py:16
  36.7 0.0 copy-start.3
  36.7 0.8 copy-done.3
  37.5 19.8 %collective-permute-done.1 = bf16[512,512]{1,0:T(8,128)(2,1)} collective-permute-done((bf16[512,512]{1,0:T(8,128)(2,1)}, bf16[512,512]{1,0:T(8,128)(2,1)}, u32[]{:S(2)}, u32[]{:S(2)}) %collective-permute-start.1) | collective-permute-done | bytes 524320 | tf_op jit(solution)/shard_map/ppermute | solution.py:16
  57.3 0.0 copy-done.1
  57.3 1.3 pad_maximum_fusion
  58.6 1.6 copy.9
  60.1 0.0 collective-permute-done.3
  60.1 0.0 copy-start.2
  60.2 0.8 copy-done.2
  61.0 0.0 collective-permute-done.2
  61.0 1.3 pad_maximum_fusion.1
  62.3 0.0 copy-start
  62.3 12.1 %fusion.28 = f32[4,2,512]{2,1,0:T(2,128)S(1)} fusion(pred[512,1536]{0,1:T(8,128)(4,1)} %fusion.9, bf16[1536,4,128,1]{0,2,3,1:T(8,128)(2,1)S(1)} %bitcast.34, bf16[512,4,2,128]{3,2,1,0:T(2,128)(2,1)} %reshape.31), kind=kOutput, calls=%fused_computation.29 | convolution fusion | flops 1642071552 | bytes 3424256 | tf_op jit(solution)/shard_map/while/body/eval_jaxpr/sub | solution.py:53
  74.4 0.0 copy-done
  74.4 16.3 %fusion.10 = bf16[4,128,2,512]{3,1,2,0:T(8,128)(2,1)} fusion(bf16[1536,4,128,1]{0,2,3,1:T(8,128)(2,1)S(1)} %bitcast.33, f32[4,2,512]{2,1,0:T(2,128)S(1)} %fusion.28, pred[512,1536]{0,1:T(8,128)(4,1)} %fusion.9, bf16[1536,4,128,1]{0,2,3,1:T(8,128)(2,1)S(1)} %bitcast.35, bf16[512,4,2,128]{3,2,1,0:T(2,128)(2,1)} %reshape.31), kind=kOutput, calls=%fused_computation.15 | convolution fusion | flops 3259504128 | bytes 6045696 | tf_op jit(solution)/shard_map/while/body/eval_jaxpr/kgqp,pkd->qkgd/dot_general | solution.py:55
  90.7 12.8 %fusion.31 = f32[512,5376]{1,0:T(8,128)} fusion(bf16[512,1024]{0,1:T(8,128)(2,1)} %bitcast.36, bf16[1024,5376]{1,0:T(8,128)(2,1)} %param.9), kind=kOutput, calls=%fused_computation.30 | convolution fusion | flops 5637144576 | bytes 23068672 | tf_op jit(solution)/shard_map/dot_general | solution.py:65
  103.5 0.0 all-gather.3.cloned.1.call-update
  103.6 38.5 %all-gather.3.cloned.1.call-done = f32[1024,5376]{1,0:T(8,128)} async-done(((f32[512,5376]{1,0:T(8,128)}), f32[1024,5376]{1,0:T(8,128)}) %all-gather.3.cloned.1.call-update) | async-done | bytes 22020112 | tf_op jit(solution)/shard_map/all_gather | solution.py:66
  142.1 12.5 %reduce_sum.20 = bf16[512,5376]{1,0:T(8,128)(2,1)} reduce(f32[2,512,5376]{2,1,0:T(8,128)} %bitcast.32, f32[]{:T(128)} %constant.47.clone.1), dimensions={0}, to_apply=%region_2.3 | reduce | flops 2752512 | bytes 27525124 | tf_op jit(solution)/shard_map/reduce_sum | solution.py:66
  (1 shorter events, 0.0 us)
Async XLA Ops:
  6.5 50.7 %copy-start.1 = (bf16[512,512]{1,0:T(8,128)(2,1)S(1)}, bf16[512,512]{1,0:T(8,128)(2,1)}, u32[]{:S(2)}) copy-start(bf16[512,512]{1,0:T(8,128)(2,1)} %param.7) | copy-start | bytes 1572868
  6.5 135.5 %all-gather.3.cloned.1.call-start = ((), (), s32[]{:S(2)}) async-start(), calls=%async_computation | async-start | bytes 33030144 | tf_op jit(solution)/shard_map/all_gather | solution.py:66
  7.9 52.3 %collective-permute-start.3 = (bf16[512,512]{0,1:T(8,128)(2,1)S(1)}, bf16[512,512]{0,1:T(8,128)(2,1)S(1)}, u32[]{:S(2)}, u32[]{:S(2)}) collective-permute-start(bf16[512,512]{0,1:T(8,128)(2,1)S(1)} %copy.10), channel_id=1, source_target_pairs={{0,2},{2,4},{4,6},{6,8},{8,10},{10,12},{12,14},{1,3},{3,5},{5,7},{... | collective-permute-start | bytes 1572872 | tf_op jit(solution)/shard_map/ppermute | solution.py:16
  11.0 50.0 %collective-permute-start.2 = (bf16[512,512]{0,1:T(8,128)(2,1)S(1)}, bf16[512,512]{0,1:T(8,128)(2,1)}, u32[]{:S(2)}, u32[]{:S(2)}) collective-permute-start(bf16[512,512]{0,1:T(8,128)(2,1)S(1)} %copy.10), channel_id=1, source_target_pairs={{0,4},{2,6},{4,8},{6,10},{8,12},{10,14},{1,5},{3,7},{5,9},{7,11},{... | collective-permute-start | bytes 1572872 | tf_op jit(solution)/shard_map/ppermute | solution.py:16
  14.2 22.4 %collective-permute-start = (bf16[512,512]{1,0:T(8,128)(2,1)}, bf16[512,512]{1,0:T(8,128)(2,1)S(1)}, u32[]{:S(2)}, u32[]{:S(2)}) collective-permute-start(bf16[512,512]{1,0:T(8,128)(2,1)} %param.7), channel_id=1, source_target_pairs={{0,4},{2,6},{4,8},{6,10},{8,12},{10,14},{1,5},{3,7},{5,9},{7,11},{... | collective-permute-start | bytes 1572872 | tf_op jit(solution)/shard_map/ppermute | solution.py:16
  16.2 41.1 %collective-permute-start.1 = (bf16[512,512]{1,0:T(8,128)(2,1)}, bf16[512,512]{1,0:T(8,128)(2,1)}, u32[]{:S(2)}, u32[]{:S(2)}) collective-permute-start(bf16[512,512]{1,0:T(8,128)(2,1)} %param.7), channel_id=1, source_target_pairs={{0,2},{2,4},{4,6},{6,8},{8,10},{10,12},{12,14},{1,3},{3,5},{5,7},{... | collective-permute-start | bytes 1572872 | tf_op jit(solution)/shard_map/ppermute | solution.py:16
  36.7 0.8 copy-start.3
  60.1 0.8 copy-start.2
  62.3 12.2 %copy-start = (bf16[1536,512]{0,1:T(8,128)(2,1)S(1)}, bf16[1536,512]{0,1:T(8,128)(2,1)}, u32[]{:S(2)}) copy-start(bf16[1536,512]{0,1:T(8,128)(2,1)} %copy.9) | copy-start | bytes 4718596
Sparse Core Ops, SparseCore 0:
  103.7 38.3 all-gather.2
